TPU v7x, 32 devices: a whole 2x2x4 slice. The times are simulated.
32 devices in a mesh: sec: 2 (over y), blk: 16 (over z, x, core).
Axes of the slice: x: 2, y: 2, z: 4, core: 2. Of those that a mesh axis runs over, the one named last changes fastest.
Arguments:
- wave_speed: float32 [2, 125, 4096], P('sec', None, 'blk'), may hold values from 0.5 to 2
- inverse_mass: float32 [2, 125, 4096], P('sec', None, 'blk'), may hold values from 0.5 to 2
- source_field: float32 [2, 125, 4096], P('sec', None, 'blk'), may hold values from -4 to 4
- source_time: float32 [2, 12], P('sec'), may hold values from -4 to 4
- face_links: int32 [2, 3, 2048], P('sec', None, 'blk'), may hold values from 0 to 255, as said below
- coupling_links: int32 [5, 8192], P(None, 'blk'), may hold values from -1 to 255, as said below
Outputs:
- adjoint_now: float32 [2, 125, 4096], P('sec', None, 'blk')
- adjoint_before: float32 [2, 125, 4096], P('sec', None, 'blk')
Inputs may be any that keep to these rules, and one draw needn't show every extreme that they name: `face_links`: in each section record k of block b and record k of its peer name each other; the peer is b XOR 2^j for a bit j that depends on the section and k only, and equals b for unlinked records, which are the trailing ones. A block's records name distinct elements. A block has at most 16 records with one peer and exactly 16 with some peer. `coupling_links`: owner -1 marks unused points, which are the trailing points of a block. A box block has at most 4 points with one owner, and every box block has exactly 4 points with one common owner.
All inputs are finite; a program needn't handle non-finite values.
Results may differ from a plain program's by a relative error of at most 0.0001.
Values sent between devices are 32-bit elements; how exact they have to be, the bound alone decides.
No kernel may reach another device: no remote copies, remote signals or barrier semaphores. Data moves between devices by JAX's collectives and lax.ppermute only.
A program may use at most 64 MiB of HBM per device.

v0:
```python
import jax
import jax.numpy as jnp
import numpy as np
from jax import lax
from jax.sharding import PartitionSpec as P

CAPC = 4
STEPS = 12
DT_SQUARED = 0.05
PENALTY = 10.0


def partner_2(value, axis, stride):
    return lax.ppermute(value, axis, [(i, i ^ 1 << stride) for i in range(lax.axis_size(axis))])


def node_tables():
    abscissae = np.array([-1.0, -np.sqrt(3.0 / 7.0), 0.0, np.sqrt(3.0 / 7.0), 1.0])
    weights = np.array([0.1, 49.0 / 90.0, 32.0 / 45.0, 49.0 / 90.0, 0.1])
    legendre = (35.0 * abscissae**4 - 30.0 * abscissae**2 + 3.0) / 8.0
    derivative = np.zeros((5, 5))
    for i in range(5):
        for j in range(5):
            if i != j:
                derivative[i, j] = legendre[i] / (legendre[j] * (abscissae[i] - abscissae[j]))
    derivative[0, 0] = -2.5
    derivative[4, 4] = 2.5
    identity = np.eye(5)
    operator = np.concatenate(
        [
            np.kron(np.kron(derivative, identity), identity),
            np.kron(np.kron(identity, derivative), identity),
            np.kron(np.kron(identity, identity), derivative),
        ],
        axis=0,
    )
    weight_cube = weights[:, None, None] * weights[None, :, None] * weights[None, None, :]
    lattice = np.arange(125).reshape(5, 5, 5)
    face_nodes = np.stack(
        [
            lattice[0].ravel(),
            lattice[4].ravel(),
            lattice[:, 0].ravel(),
            lattice[:, 4].ravel(),
            lattice[:, :, 0].ravel(),
            lattice[:, :, 4].ravel(),
        ]
    )
    return (
        operator.astype(np.float32),
        weight_cube.reshape(125, 1).astype(np.float32),
        face_nodes.astype(np.int32),
    )


def stiffness(field_in, speed_sq, operator, weight_cube):
    columns = field_in.shape[-1]
    scaling = weight_cube * speed_sq
    grads = jnp.dot(
        operator, field_in, precision=lax.Precision.HIGHEST, preferred_element_type=jnp.float32
    )
    scaled = (grads.reshape(3, 125, columns) * scaling[None]).reshape(375, columns)
    return jnp.dot(
        operator.T, scaled, precision=lax.Precision.HIGHEST, preferred_element_type=jnp.float32
    )


def body(wave_speed, inverse_mass, source_field, source_time, face_links, coupling_links):
    operator_np, weight_np, faces_np = node_tables()
    operator = jnp.asarray(operator_np)
    weight_cube = jnp.asarray(weight_np)
    picker_np = np.zeros((150, 125), np.float32)
    for side_number in range(6):
        for node_number in range(25):
            picker_np[side_number * 25 + node_number, faces_np[side_number, node_number]] = 1.0
    picker = jnp.asarray(picker_np)
    spreader = jnp.asarray(picker_np.T.copy())
    speed_sq = wave_speed[0]
    inverse = inverse_mass[0]
    forcing = source_field[0]
    timing = source_time[0]
    element = face_links[0, 0]
    face_side = face_links[0, 1]
    face_peer = face_links[0, 2]
    blocks = lax.axis_size("blk")
    bit_count = blocks.bit_length() - 1
    myself = lax.axis_index("blk")
    is_box = lax.axis_index("sec") == 0
    records = element.shape[0]
    per_peer = records // 8
    ordinal = jnp.arange(records)
    linked = face_peer != myself
    side_mask = face_side[None, None, :] == jnp.arange(6, dtype=jnp.int32)[:, None, None]
    earlier = ordinal[None, :] < ordinal[:, None]
    face_slot = jnp.sum(
        ((face_peer[:, None] == face_peer[None, :]) & earlier).astype(jnp.int32), axis=1
    )
    offset_bits = jnp.bitwise_xor(face_peer, myself)
    bit_index = jnp.zeros((records,), jnp.int32)
    for bit_number in range(bit_count):
        bit_index = bit_index + bit_number * (offset_bits == 1 << bit_number).astype(jnp.int32)
    pair_column = jnp.where(linked, bit_index * per_peer + face_slot, 0)
    point_element = coupling_links[0]
    point_node = coupling_links[1]
    point_owner = coupling_links[2]
    target_element = coupling_links[3]
    target_node = coupling_links[4]
    in_use = point_owner >= 0
    owner_safe = jnp.maximum(point_owner, 0)
    point_ordinal = jnp.arange(point_owner.shape[0])
    point_earlier = point_ordinal[None, :] < point_ordinal[:, None]
    point_slot = jnp.sum(
        ((point_owner[:, None] == point_owner[None, :]) & point_earlier).astype(jnp.int32), axis=1
    )
    point_column = jnp.where(in_use, point_slot * blocks + owner_safe, 0)
    slot_total = CAPC * blocks
    outbound = jnp.zeros((3, slot_total), jnp.int32)
    outbound = outbound.at[0, point_column].add(jnp.where(in_use, target_element, 0))
    outbound = outbound.at[1, point_column].add(jnp.where(in_use, target_node, 0))
    outbound = outbound.at[2, point_column].add(in_use.astype(jnp.int32))
    inbound = lax.all_to_all(
        outbound.reshape(3, CAPC, blocks), "blk", split_axis=2, concat_axis=2, tiled=True
    ).reshape(3, slot_total)
    remote_element = inbound[0]
    remote_node = inbound[1]
    remote_flag = inbound[2].astype(jnp.float32)
    target_rows = jnp.concatenate([point_node, remote_node])
    target_cols = jnp.concatenate([point_element, remote_element])
    current = jnp.zeros(speed_sq.shape, jnp.float32)
    previous = jnp.zeros(speed_sq.shape, jnp.float32)
    for moment in range(STEPS):
        internal = stiffness(current, speed_sq, operator, weight_cube)
        stacked = jnp.dot(
            picker,
            internal[:, element],
            precision=lax.Precision.HIGHEST,
            preferred_element_type=jnp.float32,
        ).reshape(6, 25, records)
        payload = jnp.sum(jnp.where(side_mask, stacked, 0.0), axis=0)
        payload = jnp.where(linked[None, :], payload, 0.0)
        outgoing = (
            jnp.zeros((25, bit_count * per_peer), jnp.float32).at[:, pair_column].add(payload)
        )
        arrived = []
        for bit_number in range(bit_count):
            piece = outgoing[:, bit_number * per_peer : (bit_number + 1) * per_peer]
            arrived.append(partner_2(piece, "blk", bit_number))
        partner = jnp.concatenate(arrived, axis=1)[:, pair_column]
        partner = jnp.where(linked[None, :], partner, 0.0)
        masked = jnp.where(side_mask, partner[None], 0.0).reshape(150, records)
        assembled = internal.at[:, element].add(
            jnp.dot(
                spreader,
                masked,
                precision=lax.Precision.HIGHEST,
                preferred_element_type=jnp.float32,
            )
        )
        velocity = current - previous
        traction = assembled[point_node, point_element]
        box_send = (
            jnp.zeros((slot_total,), jnp.float32)
            .at[point_column]
            .add(jnp.where(in_use, traction, 0.0))
        )
        global_send = velocity[remote_node, remote_element] * remote_flag
        dispatch = jnp.where(is_box, box_send, global_send).reshape(CAPC, blocks)
        crossed = partner_2(dispatch, "sec", 0)
        received = lax.all_to_all(crossed, "blk", split_axis=1, concat_axis=1, tiled=True)
        received = received.reshape(slot_total)
        remote_velocity = received[point_column]
        box_terms = jnp.where(
            in_use, PENALTY * (remote_velocity - velocity[point_node, point_element]), 0.0
        )
        values = jnp.concatenate(
            [jnp.where(is_box, box_terms, 0.0), jnp.where(is_box, 0.0, received * remote_flag)]
        )
        driving = timing[moment] * forcing - assembled
        driving = driving.at[target_rows, target_cols].add(values)
        advanced = 2.0 * current - previous + DT_SQUARED * inverse * driving
        previous = current
        current = advanced
    return (current[None], previous[None])


def solution(mesh):
    in_specs = (
        P("sec", None, "blk"),
        P("sec", None, "blk"),
        P("sec", None, "blk"),
        P("sec", None),
        P("sec", None, "blk"),
        P(None, "blk"),
    )
    out_specs = (P("sec", None, "blk"), P("sec", None, "blk"))
    return jax.shard_map(body, mesh=mesh, in_specs=in_specs, out_specs=out_specs, check_vma=False)
```

profile of v0, /device:TPU:0, one launch (start us, length us, event | category | flops | bytes accessed | tf_op | source)
XLA Modules:
  0.0 1408.7 jit_solution(6198110718570769417)
XLA Ops:
  24.5 22.8 %scatter_fusion.1 = s32[3,64]{1,0:T(4,128)S(1)} fusion(s32[3,64]{1,0:T(4,128)S(1)} %broadcast_in_dim.578, s32[512]{0:T(512)S(1)} %bitcast.1117, s32[512]{0:T(512)S(1)} %get-tuple-element.946), kind=kCustom, calls=%fused_computation.62 | custom fusion | flops 512 | bytes 10240 | tf_op jit(solution)/shard_map/scatter-add | solution.py:118
  47.3 22.8 %scatter_fusion.2 = s32[3,64]{1,0:T(4,128)S(1)} fusion(s32[3,64]{1,0:T(4,128)S(1)} %scatter_fusion.1, s32[512]{0:T(512)S(1)} %bitcast.1116, s32[512]{0:T(512)S(1)} %get-tuple-element.945), kind=kCustom, calls=%fused_computation.63 | custom fusion | flops 512 | bytes 10240 | tf_op jit(solution)/shard_map/scatter-add | solution.py:119
  70.0 22.8 %scatter_fusion.3 = s32[3,64]{1,0:T(4,128)S(1)} fusion(s32[3,64]{1,0:T(4,128)S(1)} %scatter_fusion.2, s32[512]{0:T(512)S(1)} %bitcast.1115, s32[512]{0:T(512)S(1)} %convert_element_type.31), kind=kCustom, calls=%fused_computation.64 | custom fusion | flops 512 | bytes 10240 | tf_op jit(solution)/shard_map/scatter-add | solution.py:120
  112.4 6.2 all-to-all-start.1
  118.6 6.3 all-to-all-done.1
  128.0 40.1 %fusion.83 = (f32[512]{0:T(512)S(1)}, pred[512]{0:T(512)(128)(4,1)S(1)}, pred[512]{0:T(512)(128)(4,1)S(1)}, pred[512]{0:T(512)(128)(4,1)S(1)}, pred[512]{0:T(512...) fusion(pred[512]{0:T(512)(128)(4,1)S(1)} %get-tuple-element.99,, ...), kind=kLoop, calls=%fused_computation.341 | loop fusion | flops 66560 | bytes 39169 | tf_op jit(solution)/shard_map/jit(_where)/select_n | solution.py:176
  168.1 30.1 %scatter_fusion.4 = f32[125,256]{1,0:T(8,128)S(1)} fusion(f32[125,256]{1,0:T(8,128)S(1)} %copy.421, s32[576]{0:T(1024)S(1)} %fusion.42, f32[576]{0:T(1024)S(1)} %pad_maximum_fusion.12), kind=kCustom, calls=%fused_computation.66 | custom fusion | flops 576 | bytes 11520 | tf_op jit(solution)/shard_map/scatter-add | solution.py:179
  229.7 5.5 all-to-all-done.2
  238.2 40.1 %fusion.80 = f32[512]{0:T(512)S(1)} fusion(pred[512]{0:T(512)(128)(4,1)S(1)} %get-tuple-element.99, f32[512]{0:T(512)S(1)} %gather_fusion.9, pred[512]{0:T(512)(128)(4,1)S(1)} %get-tuple-element.97, pred[512]{0:T(512)(128)(4,1)S(1)} %get-tuple-element.96, pred[512]{0:T(512)(128)(4,1)S(1)} %get-tuple-element.95, pred[512]{0:T(512)(128)(4,1)S(1)} %get-tuple-element.94, ...), kind=kLoop, calls=%fused_computation.337 | loop fusion | flops 34304 | bytes 37121 | tf_op jit(solution)/shard_map/jit(_where)/select_n | solution.py:176
  278.3 30.1 %scatter_fusion.6 = f32[125,256]{1,0:T(8,128)S(1)} fusion(f32[125,256]{1,0:T(8,128)S(1)} %copy.429, s32[576]{0:T(1024)S(1)} %fusion.42, f32[576]{0:T(1024)S(1)} %pad_maximum_fusion.13), kind=kCustom, calls=%fused_computation.70 | custom fusion | flops 576 | bytes 11520 | tf_op jit(solution)/shard_map/scatter-add | solution.py:179
  339.2 5.6 all-to-all-done.3
  347.8 40.0 %fusion.77 = f32[512]{0:T(512)S(1)} fusion(pred[512]{0:T(512)(128)(4,1)S(1)} %get-tuple-element.99, f32[512]{0:T(512)S(1)} %gather_fusion.14, pred[512]{0:T(512)(128)(4,1)S(1)} %get-tuple-element.97, pred[512]{0:T(512)(128)(4,1)S(1)} %get-tuple-element.96, pred[512]{0:T(512)(128)(4,1)S(1)} %get-tuple-element.95, pred[512]{0:T(512)(128)(4,1)S(1)} %get-tuple-element.94, ...), kind=kLoop, calls=%fused_computation.333 | loop fusion | flops 34304 | bytes 37121 | tf_op jit(solution)/shard_map/jit(_where)/select_n | solution.py:176
  387.9 30.1 %scatter_fusion.8 = f32[125,256]{1,0:T(8,128)S(1)} fusion(f32[125,256]{1,0:T(8,128)S(1)} %copy.437, s32[576]{0:T(1024)S(1)} %fusion.42, f32[576]{0:T(1024)S(1)} %pad_maximum_fusion.14), kind=kCustom, calls=%fused_computation.74 | custom fusion | flops 576 | bytes 11520 | tf_op jit(solution)/shard_map/scatter-add | solution.py:179
  444.0 4.9 all-to-all-start.4
  449.7 5.5 all-to-all-done.4
  458.2 40.1 %fusion.74 = f32[512]{0:T(512)S(1)} fusion(pred[512]{0:T(512)(128)(4,1)S(1)} %get-tuple-element.99, f32[512]{0:T(512)S(1)} %gather_fusion.19, pred[512]{0:T(512)(128)(4,1)S(1)} %get-tuple-element.97, pred[512]{0:T(512)(128)(4,1)S(1)} %get-tuple-element.96, pred[512]{0:T(512)(128)(4,1)S(1)} %get-tuple-element.95, pred[512]{0:T(512)(128)(4,1)S(1)} %get-tuple-element.94, ...), kind=kLoop, calls=%fused_computation.329 | loop fusion | flops 34304 | bytes 37121 | tf_op jit(solution)/shard_map/jit(_where)/select_n | solution.py:176
  498.3 30.1 %scatter_fusion.10 = f32[125,256]{1,0:T(8,128)S(1)} fusion(f32[125,256]{1,0:T(8,128)S(1)} %copy.445, s32[576]{0:T(1024)S(1)} %fusion.42, f32[576]{0:T(1024)S(1)} %pad_maximum_fusion.15), kind=kCustom, calls=%fused_computation.78 | custom fusion | flops 576 | bytes 11520 | tf_op jit(solution)/shard_map/scatter-add | solution.py:179
  553.3 4.7 all-to-all-start.5
  558.7 5.6 all-to-all-done.5
  567.4 39.9 %fusion.71 = f32[512]{0:T(512)S(1)} fusion(pred[512]{0:T(512)(128)(4,1)S(1)} %get-tuple-element.99, f32[512]{0:T(512)S(1)} %gather_fusion.24, pred[512]{0:T(512)(128)(4,1)S(1)} %get-tuple-element.97, pred[512]{0:T(512)(128)(4,1)S(1)} %get-tuple-element.96, pred[512]{0:T(512)(128)(4,1)S(1)} %get-tuple-element.95, pred[512]{0:T(512)(128)(4,1)S(1)} %get-tuple-element.94, ...), kind=kLoop, calls=%fused_computation.325 | loop fusion | flops 34304 | bytes 37121 | tf_op jit(solution)/shard_map/jit(_where)/select_n | solution.py:176
  607.4 30.1 %scatter_fusion.12 = f32[125,256]{1,0:T(8,128)S(1)} fusion(f32[125,256]{1,0:T(8,128)S(1)} %copy.453, s32[576]{0:T(1024)S(1)} %fusion.42, f32[576]{0:T(1024)S(1)} %pad_maximum_fusion.16), kind=kCustom, calls=%fused_computation.82 | custom fusion | flops 576 | bytes 11520 | tf_op jit(solution)/shard_map/scatter-add | solution.py:179
  663.7 4.7 all-to-all-start.6
  669.1 5.6 all-to-all-done.6
  677.7 40.0 %fusion.68 = f32[512]{0:T(512)S(1)} fusion(pred[512]{0:T(512)(128)(4,1)S(1)} %get-tuple-element.99, f32[512]{0:T(512)S(1)} %gather_fusion.29, pred[512]{0:T(512)(128)(4,1)S(1)} %get-tuple-element.97, pred[512]{0:T(512)(128)(4,1)S(1)} %get-tuple-element.96, pred[512]{0:T(512)(128)(4,1)S(1)} %get-tuple-element.95, pred[512]{0:T(512)(128)(4,1)S(1)} %get-tuple-element.94, ...), kind=kLoop, calls=%fused_computation.321 | loop fusion | flops 34304 | bytes 37121 | tf_op jit(solution)/shard_map/jit(_where)/select_n | solution.py:176
  717.8 30.1 %scatter_fusion.14 = f32[125,256]{1,0:T(8,128)S(1)} fusion(f32[125,256]{1,0:T(8,128)S(1)} %copy.461, s32[576]{0:T(1024)S(1)} %fusion.42, f32[576]{0:T(1024)S(1)} %pad_maximum_fusion.17), kind=kCustom, calls=%fused_computation.86 | custom fusion | flops 576 | bytes 11520 | tf_op jit(solution)/shard_map/scatter-add | solution.py:179
  772.8 5.1 all-to-all-start.7
  778.7 5.6 all-to-all-done.7
  787.3 40.0 %fusion.65 = f32[512]{0:T(512)S(1)} fusion(pred[512]{0:T(512)(128)(4,1)S(1)} %get-tuple-element.99, f32[512]{0:T(512)S(1)} %gather_fusion.34, pred[512]{0:T(512)(128)(4,1)S(1)} %get-tuple-element.97, pred[512]{0:T(512)(128)(4,1)S(1)} %get-tuple-element.96, pred[512]{0:T(512)(128)(4,1)S(1)} %get-tuple-element.95, pred[512]{0:T(512)(128)(4,1)S(1)} %get-tuple-element.94, ...), kind=kLoop, calls=%fused_computation.317 | loop fusion | flops 34304 | bytes 37121 | tf_op jit(solution)/shard_map/jit(_where)/select_n | solution.py:176
  827.3 30.1 %scatter_fusion.16 = f32[125,256]{1,0:T(8,128)S(1)} fusion(f32[125,256]{1,0:T(8,128)S(1)} %copy.469, s32[576]{0:T(1024)S(1)} %fusion.42, f32[576]{0:T(1024)S(1)} %pad_maximum_fusion.18), kind=kCustom, calls=%fused_computation.90 | custom fusion | flops 576 | bytes 11520 | tf_op jit(solution)/shard_map/scatter-add | solution.py:179
  883.4 4.7 all-to-all-start.8
  888.9 5.6 all-to-all-done.8
  897.5 40.0 %fusion.62 = f32[512]{0:T(512)S(1)} fusion(pred[512]{0:T(512)(128)(4,1)S(1)} %get-tuple-element.99, f32[512]{0:T(512)S(1)} %gather_fusion.39, pred[512]{0:T(512)(128)(4,1)S(1)} %get-tuple-element.97, pred[512]{0:T(512)(128)(4,1)S(1)} %get-tuple-element.96, pred[512]{0:T(512)(128)(4,1)S(1)} %get-tuple-element.95, pred[512]{0:T(512)(128)(4,1)S(1)} %get-tuple-element.94, ...), kind=kLoop, calls=%fused_computation.313 | loop fusion | flops 34304 | bytes 37121 | tf_op jit(solution)/shard_map/jit(_where)/select_n | solution.py:176
  937.5 30.1 %scatter_fusion.18 = f32[125,256]{1,0:T(8,128)S(1)} fusion(f32[125,256]{1,0:T(8,128)S(1)} %copy.477, s32[576]{0:T(1024)S(1)} %fusion.42, f32[576]{0:T(1024)S(1)} %pad_maximum_fusion.19), kind=kCustom, calls=%fused_computation.94 | custom fusion | flops 576 | bytes 11520 | tf_op jit(solution)/shard_map/scatter-add | solution.py:179
  992.7 4.7 all-to-all-start.9
  998.2 5.6 all-to-all-done.9
  1006.8 40.0 %fusion.59 = f32[512]{0:T(512)S(1)} fusion(pred[512]{0:T(512)(128)(4,1)S(1)} %get-tuple-element.99, f32[512]{0:T(512)S(1)} %gather_fusion.44, pred[512]{0:T(512)(128)(4,1)S(1)} %get-tuple-element.97, pred[512]{0:T(512)(128)(4,1)S(1)} %get-tuple-element.96, pred[512]{0:T(512)(128)(4,1)S(1)} %get-tuple-element.95, pred[512]{0:T(512)(128)(4,1)S(1)} %get-tuple-element.94, ...), kind=kLoop, calls=%fused_computation.309 | loop fusion | flops 34304 | bytes 37121 | tf_op jit(solution)/shard_map/jit(_where)/select_n | solution.py:176
  1046.9 30.1 %scatter_fusion.20 = f32[125,256]{1,0:T(8,128)S(1)} fusion(f32[125,256]{1,0:T(8,128)S(1)} %copy.485, s32[576]{0:T(1024)S(1)} %fusion.42, f32[576]{0:T(1024)S(1)} %pad_maximum_fusion.20), kind=kCustom, calls=%fused_computation.98 | custom fusion | flops 576 | bytes 11520 | tf_op jit(solution)/shard_map/scatter-add | solution.py:179
  1102.9 4.9 all-to-all-start.10
  1108.6 5.5 all-to-all-done.10
  1117.2 40.0 %fusion.56 = f32[512]{0:T(512)S(1)} fusion(pred[512]{0:T(512)(128)(4,1)S(1)} %get-tuple-element.99, f32[512]{0:T(512)S(1)} %gather_fusion.49, pred[512]{0:T(512)(128)(4,1)S(1)} %get-tuple-element.97, pred[512]{0:T(512)(128)(4,1)S(1)} %get-tuple-element.96, pred[512]{0:T(512)(128)(4,1)S(1)} %get-tuple-element.95, pred[512]{0:T(512)(128)(4,1)S(1)} %get-tuple-element.94, ...), kind=kLoop, calls=%fused_computation.305 | loop fusion | flops 34304 | bytes 37121 | tf_op jit(solution)/shard_map/jit(_where)/select_n | solution.py:176
  1157.2 30.1 %scatter_fusion.22 = f32[125,256]{1,0:T(8,128)S(1)} fusion(f32[125,256]{1,0:T(8,128)S(1)} %copy.493, s32[576]{0:T(1024)S(1)} %fusion.42, f32[576]{0:T(1024)S(1)} %pad_maximum_fusion.21), kind=kCustom, calls=%fused_computation.102 | custom fusion | flops 576 | bytes 11520 | tf_op jit(solution)/shard_map/scatter-add | solution.py:179
  1212.3 4.7 all-to-all-start.11
  1217.7 5.6 all-to-all-done.11
  1226.4 39.9 %fusion.53 = f32[512]{0:T(512)S(1)} fusion(pred[512]{0:T(512)(128)(4,1)S(1)} %get-tuple-element.99, f32[512]{0:T(512)S(1)} %gather_fusion.54, pred[512]{0:T(512)(128)(4,1)S(1)} %get-tuple-element.97, pred[512]{0:T(512)(128)(4,1)S(1)} %get-tuple-element.96, pred[512]{0:T(512)(128)(4,1)S(1)} %get-tuple-element.95, pred[512]{0:T(512)(128)(4,1)S(1)} %get-tuple-element.94, ...), kind=kLoop, calls=%fused_computation.301 | loop fusion | flops 34304 | bytes 37121 | tf_op jit(solution)/shard_map/jit(_where)/select_n | solution.py:176
  1266.2 30.1 %scatter_fusion.24 = f32[125,256]{1,0:T(8,128)S(1)} fusion(f32[125,256]{1,0:T(8,128)S(1)} %copy.501, s32[576]{0:T(1024)S(1)} %fusion.42, f32[576]{0:T(1024)S(1)} %pad_maximum_fusion.22), kind=kCustom, calls=%fused_computation.106 | custom fusion | flops 576 | bytes 11520 | tf_op jit(solution)/shard_map/scatter-add | solution.py:179
  1328.9 5.5 all-to-all-done.12
  1337.4 39.9 %fusion.50 = f32[512]{0:T(512)S(1)} fusion(pred[512]{0:T(512)(128)(4,1)S(1)} %get-tuple-element.99, f32[512]{0:T(512)S(1)} %gather_fusion.59, pred[512]{0:T(512)(128)(4,1)S(1)} %get-tuple-element.97, pred[512]{0:T(512)(128)(4,1)S(1)} %get-tuple-element.96, pred[512]{0:T(512)(128)(4,1)S(1)} %get-tuple-element.95, pred[512]{0:T(512)(128)(4,1)S(1)} %get-tuple-element.94, ...), kind=kLoop, calls=%fused_computation.297 | loop fusion | flops 34304 | bytes 37121 | tf_op jit(solution)/shard_map/jit(_where)/select_n | solution.py:176
  1377.3 30.1 %scatter_fusion.26 = f32[125,256]{1,0:T(8,128)S(1)} fusion(f32[125,256]{1,0:T(8,128)S(1)} %copy.509, s32[576]{0:T(1024)S(1)} %fusion.42, f32[576]{0:T(1024)S(1)} %pad_maximum_fusion.23), kind=kCustom, calls=%fused_computation.110 | custom fusion | flops 576 | bytes 11520 | tf_op jit(solution)/shard_map/scatter-add | solution.py:179
  (622 shorter events, 383.1 us)
Async XLA Ops:
  7.8 7.6 collective-permute-start
  8.3 7.1 collective-permute-start.3
  93.6 13.0 all-to-all-start
  112.4 12.6 all-to-all-start.1
  202.1 4.6 collective-permute-start.8
  202.6 4.1 collective-permute-start.7
  217.5 6.0 collective-permute-start.9
  224.2 11.0 all-to-all-start.2
  312.7 4.7 collective-permute-start.13
  313.3 4.1 collective-permute-start.12
  328.1 5.0 collective-permute-start.14
  333.8 11.0 all-to-all-start.3
  421.9 4.6 collective-permute-start.18
  422.4 4.1 collective-permute-start.17
  437.2 6.0 collective-permute-start.19
  444.0 11.2 all-to-all-start.4
  532.3 4.6 collective-permute-start.23
  532.8 4.1 collective-permute-start.22
  547.6 5.0 collective-permute-start.24
  553.3 11.0 all-to-all-start.5
  641.6 4.6 collective-permute-start.28
  642.2 4.1 collective-permute-start.27
  656.9 6.0 collective-permute-start.29
  663.7 11.0 all-to-all-start.6
  751.7 4.6 collective-permute-start.33
  752.3 4.1 collective-permute-start.32
  767.1 5.0 collective-permute-start.34
  772.8 11.4 all-to-all-start.7
  861.3 4.6 collective-permute-start.38
  861.9 4.1 collective-permute-start.37
  876.7 6.1 collective-permute-start.39
  883.4 11.0 all-to-all-start.8
  971.6 4.7 collective-permute-start.43
  972.2 4.1 collective-permute-start.42
  987.0 5.0 collective-permute-start.44
  992.7 11.0 all-to-all-start.9
  1080.8 4.7 collective-permute-start.48
  1081.4 4.1 collective-permute-start.47
  1096.2 6.0 collective-permute-start.49
  1102.9 11.2 all-to-all-start.10
  1191.2 4.7 collective-permute-start.53
  1191.8 4.1 collective-permute-start.52
  1206.6 5.0 collective-permute-start.54
  1212.3 11.0 all-to-all-start.11
  1300.5 4.7 collective-permute-start.58
  1301.1 4.1 collective-permute-start.57
  1315.8 6.8 collective-permute-start.59
  1323.4 11.0 all-to-all-start.12
  (34 other events, 154.4 us)
where the time goes:
time: 1420 us; the launch traced here: 1410 us
  other arithmetic  1000 us (70%)
  local copies, waits for them, and re-layouts  181 us (13%)
  starting transfers between devices  102 us (7%)
  waiting for transfers between devices  94.7 us (7%)
  matrix products  23.8 us (2%)
    select_n x12, other arithmetic, body(): jnp.where(is_box, box_terms, 0.0)  480 us
    scatter-add x12, other arithmetic, body(): driving = driving.at[target_rows, target_cols].add(values)  362 us
    all_to_all x12, waiting for transfers between devices, body(): lax.all_to_all(crossed, 'blk', split_axis=1, concat_axis=1, tiled=True)  67.6 us
    all_to_all x12, starting transfers between devices, body(): lax.all_to_all(crossed, 'blk', split_axis=1, concat_axis=1, tiled=True)  58.6 us
    gather x12, local copies, waits for them, and re-layouts, body(): velocity[point_node, point_element]  54.2 us
    scatter-add x12, other arithmetic, body(): box_send = jnp.zeros((slot_total,), jnp.float32).at[point_column].add(jnp...  49 us
    gather x12, local copies, waits for them, and re-layouts, body(): traction = assembled[point_node, point_element]  45 us
    ppermute x60, starting transfers between devices, partner_2(): lax.ppermute(value, axis, [(i, i ^ 1 << stride) for i in range(lax.axis_s...  40.2 us
  transfers between devices with their start and end apart: 73, of which 37 were waited for; matrix products, arithmetic and copies ran while one was open for 6% of the time, Pallas kernels for 0%

commit v1 on v0

--- a/solution.py
+++ b/solution.py
@@ -8,6 +8,20 @@
 STEPS = 12
 DT_SQUARED = 0.05
 PENALTY = 10.0
+
+
+def end_groups_now(in_array, array_dim, a0):
+    before = in_array.shape
+    d_next = in_array.reshape(
+        *before[:array_dim], a0, before[array_dim] // a0, *before[array_dim + 1 :]
+    )
+    return jnp.moveaxis(d_next, array_dim, 0)
+
+
+def push_the_wall(buf, d_out):
+    buf = jnp.moveaxis(buf, 0, d_out)
+    later = buf.shape
+    return buf.reshape(*later[:d_out], later[d_out] * later[d_out + 1], *later[d_out + 2 :])
 
 
 def partner_2(value, axis, stride):
@@ -166,7 +180,18 @@
         global_send = velocity[remote_node, remote_element] * remote_flag
         dispatch = jnp.where(is_box, box_send, global_send).reshape(CAPC, blocks)
         crossed = partner_2(dispatch, "sec", 0)
-        received = lax.all_to_all(crossed, "blk", split_axis=1, concat_axis=1, tiled=True)
+        r_now, mixed_arr = (lax.axis_size("blk"), lax.axis_index("blk"))
+        w1 = end_groups_now(crossed, 1, r_now)
+        b_now = w1
+        for to_i in range(1, r_now):
+            u_next, val = ((mixed_arr + to_i) % r_now, (mixed_arr - to_i) % r_now)
+            tall = lax.dynamic_index_in_dim(w1, u_next, 0)
+            column = []
+            for hop_no in range(r_now):
+                column.append((hop_no, (hop_no + to_i) % r_now))
+            z1 = lax.ppermute(tall, "blk", column)
+            b_now = lax.dynamic_update_slice_in_dim(b_now, z1, val, axis=0)
+        received = push_the_wall(b_now, 1)
         received = received.reshape(slot_total)
         remote_velocity = received[point_column]
         box_terms = jnp.where(

time: 1420 us -> 2530 us (1.78)
  waiting for transfers between devices: 94.7 us -> 495 us
  other arithmetic: 1000 us -> 1400 us
  local copies, waits for them, and re-layouts: 181 us -> 404 us
  starting transfers between devices: 102 us -> 159 us
    ppermute x0 -> x180, waiting for transfers between devices: none -> 488 us  [body(): z1 = lax.ppermute(tall, 'blk', column)]
    scatter-add x12, other arithmetic: 362 us -> 737 us  [body(): driving = driving.at[target_rows, target_cols].add(values)]
    dynamic_update_slice x0 -> x180, local copies, waits for them, and re-layouts: none -> 187 us  [body(): b_now = lax.dynamic_update_slice_in_dim(b_now, z1, val, axis=0)]
    all_to_all x12 -> x0, waiting for transfers between devices: 67.6 us -> none  [body(): lax.all_to_all(crossed, 'blk', split_axis=1, concat_axis=1, tiled=True)]
    ppermute x0 -> x180, starting transfers between devices: none -> 65.2 us  [body(): z1 = lax.ppermute(tall, 'blk', column)]
    all_to_all x12 -> x0, starting transfers between devices: 58.6 us -> none  [body(): lax.all_to_all(crossed, 'blk', split_axis=1, concat_axis=1, tiled=True)]
    ppermute x60, starting transfers between devices: 40.2 us -> 90.2 us  [partner_2(): lax.ppermute(value, axis, [(i, i ^ 1 << stride) for i in range(lax.axis_s...]
  transfers between devices with their start and end apart: 73 -> 241, of which waited for: 37 -> 139; matrix products, arithmetic and copies ran while one was open for 6% -> 11% of each run, Pallas kernels for 0% -> 0%
where the time goes in v1:
time: 2530 us; the launch traced here: 2500 us
  other arithmetic  1400 us (55%)
  waiting for transfers between devices  495 us (20%)
  local copies, waits for them, and re-layouts  404 us (16%)
  starting transfers between devices  159 us (6%)
  matrix products  30.5 us (1%)
    scatter-add x12, other arithmetic, body(): driving = driving.at[target_rows, target_cols].add(values)  737 us
    ppermute x180, waiting for transfers between devices, body(): z1 = lax.ppermute(tall, 'blk', column)  488 us
    select_n x12, other arithmetic, body(): jnp.where(is_box, box_terms, 0.0)  476 us
    dynamic_update_slice x180, local copies, waits for them, and re-layouts, body(): b_now = lax.dynamic_update_slice_in_dim(b_now, z1, val, axis=0)  187 us
    ppermute x60, starting transfers between devices, partner_2(): lax.ppermute(value, axis, [(i, i ^ 1 << stride) for i in range(lax.axis_s...  90.2 us
    ppermute x180, starting transfers between devices, body(): z1 = lax.ppermute(tall, 'blk', column)  65.2 us
    gather x12, local copies, waits for them, and re-layouts, body(): velocity[point_node, point_element]  54.2 us
    gather x12, local copies, waits for them, and re-layouts, body(): traction = assembled[point_node, point_element]  52.5 us
  transfers between devices with their start and end apart: 241, of which 139 were waited for; matrix products, arithmetic and copies ran while one was open for 11% of the time, Pallas kernels for 0%

profile of v1, /device:TPU:0, one launch (start us, length us, event | category | flops | bytes accessed | tf_op | source)
XLA Modules:
  0.0 2497.3 jit_solution(220404514875286184)
XLA Ops:
  29.0 22.8 scatter_fusion.1
  51.8 22.8 scatter_fusion.2
  74.5 22.8 scatter_fusion.3
  117.3 5.6 collective-permute-done.5
  123.1 6.2 collective-permute-done.6
  134.1 5.3 collective-permute-done.8
  144.3 5.3 collective-permute-done.10
  173.2 39.7 %fusion.263 = (f32[512]{0:T(512)S(1)}, pred[512]{0:T(512)(128)(4,1)S(1)}, pred[512]{0:T(512)(128)(4,1)S(1)}, pred[512]{0:T(512)(128)(4,1)S(1)}, pred[512]{0:T(51...) fusion(pred[512]{0:T(512)(128)(4,1)S(1)} %get-tuple-element.99,, ...), kind=kLoop, calls=%fused_computation.701 | loop fusion | flops 66560 | bytes 39169 | tf_op jit(solution)/shard_map/jit(_where)/select_n | solution.py:201
  212.9 30.1 %scatter_fusion.4 = f32[125,256]{1,0:T(8,128)S(1)} fusion(f32[125,256]{1,0:T(8,128)S(1)} %copy.1286, s32[576]{0:T(1024)S(1)} %fusion.42, f32[576]{0:T(1024)S(1)} %pad_maximum_fusion.12), kind=kCustom, calls=%fused_computation.66 | custom fusion | flops 576 | bytes 11520 | tf_op jit(solution)/shard_map/scatter-add | solution.py:204
  276.6 5.7 collective-permute-done.25
  282.4 6.2 collective-permute-done.26
  293.5 5.3 collective-permute-done.28
  303.7 5.3 collective-permute-done.30
  332.2 39.6 %fusion.260 = f32[512]{0:T(512)S(1)} fusion(pred[512]{0:T(512)(128)(4,1)S(1)} %get-tuple-element.99, f32[512]{0:T(512)S(1)} %gather_fusion.9, pred[512]{0:T(512)(128)(4,1)S(1)} %get-tuple-element.97, pred[512]{0:T(512)(128)(4,1)S(1)} %get-tuple-element.96, pred[512]{0:T(512)(128)(4,1)S(1)} %get-tuple-element.95, pred[512]{0:T(512)(128)(4,1)S(1)} %get-tuple-element.94, ...), kind=kLoop, calls=%fused_computation.697 | loop fusion | flops 34304 | bytes 37121 | tf_op jit(solution)/shard_map/jit(_where)/select_n | solution.py:201
  371.9 30.1 %scatter_fusion.6 = f32[125,256]{1,0:T(8,128)S(1)} fusion(f32[125,256]{1,0:T(8,128)S(1)} %copy.1307, s32[576]{0:T(1024)S(1)} %fusion.42, f32[576]{0:T(1024)S(1)} %pad_maximum_fusion.13), kind=kCustom, calls=%fused_computation.70 | custom fusion | flops 576 | bytes 11520 | tf_op jit(solution)/shard_map/scatter-add | solution.py:204
  441.9 5.0 collective-permute-done.45
  503.9 39.5 %fusion.257 = f32[512]{0:T(512)S(1)} fusion(pred[512]{0:T(512)(128)(4,1)S(1)} %get-tuple-element.99, f32[512]{0:T(512)S(1)} %gather_fusion.14, pred[512]{0:T(512)(128)(4,1)S(1)} %get-tuple-element.97, pred[512]{0:T(512)(128)(4,1)S(1)} %get-tuple-element.96, pred[512]{0:T(512)(128)(4,1)S(1)} %get-tuple-element.95, pred[512]{0:T(512)(128)(4,1)S(1)} %get-tuple-element.94, ...), kind=kLoop, calls=%fused_computation.693 | loop fusion | flops 34304 | bytes 37121 | tf_op jit(solution)/shard_map/jit(_where)/select_n | solution.py:201
  543.4 71.9 %scatter_fusion.8 = f32[125,256]{1,0:T(8,128)} fusion(f32[125,256]{1,0:T(8,128)} %copy.1328, s32[576]{0:T(1024)S(1)} %fusion.42, f32[576]{0:T(1024)S(1)} %pad_maximum_fusion.14), kind=kCustom, calls=%fused_computation.74 | custom fusion | flops 576 | bytes 11520 | tf_op jit(solution)/shard_map/scatter-add | solution.py:204
  656.2 5.1 collective-permute-done.65
  718.3 39.5 %fusion.254 = f32[512]{0:T(512)S(1)} fusion(pred[512]{0:T(512)(128)(4,1)S(1)} %get-tuple-element.99, f32[512]{0:T(512)S(1)} %gather_fusion.19, pred[512]{0:T(512)(128)(4,1)S(1)} %get-tuple-element.97, pred[512]{0:T(512)(128)(4,1)S(1)} %get-tuple-element.96, pred[512]{0:T(512)(128)(4,1)S(1)} %get-tuple-element.95, pred[512]{0:T(512)(128)(4,1)S(1)} %get-tuple-element.94, ...), kind=kLoop, calls=%fused_computation.689 | loop fusion | flops 34304 | bytes 37121 | tf_op jit(solution)/shard_map/jit(_where)/select_n | solution.py:201
  757.8 71.9 %scatter_fusion.10 = f32[125,256]{1,0:T(8,128)} fusion(f32[125,256]{1,0:T(8,128)} %copy.1349, s32[576]{0:T(1024)S(1)} %fusion.42, f32[576]{0:T(1024)S(1)} %pad_maximum_fusion.15), kind=kCustom, calls=%fused_computation.78 | custom fusion | flops 576 | bytes 11520 | tf_op jit(solution)/shard_map/scatter-add | solution.py:204
  870.7 5.0 collective-permute-done.85
  932.9 39.5 %fusion.251 = f32[512]{0:T(512)S(1)} fusion(pred[512]{0:T(512)(128)(4,1)S(1)} %get-tuple-element.99, f32[512]{0:T(512)S(1)} %gather_fusion.24, pred[512]{0:T(512)(128)(4,1)S(1)} %get-tuple-element.97, pred[512]{0:T(512)(128)(4,1)S(1)} %get-tuple-element.96, pred[512]{0:T(512)(128)(4,1)S(1)} %get-tuple-element.95, pred[512]{0:T(512)(128)(4,1)S(1)} %get-tuple-element.94, ...), kind=kLoop, calls=%fused_computation.685 | loop fusion | flops 34304 | bytes 37121 | tf_op jit(solution)/shard_map/jit(_where)/select_n | solution.py:201
  972.5 71.9 %scatter_fusion.12 = f32[125,256]{1,0:T(8,128)} fusion(f32[125,256]{1,0:T(8,128)} %copy.1370, s32[576]{0:T(1024)S(1)} %fusion.42, f32[576]{0:T(1024)S(1)} %pad_maximum_fusion.16), kind=kCustom, calls=%fused_computation.82 | custom fusion | flops 576 | bytes 11520 | tf_op jit(solution)/shard_map/scatter-add | solution.py:204
  1085.2 5.2 collective-permute-done.105
  1147.3 39.5 %fusion.248 = f32[512]{0:T(512)S(1)} fusion(pred[512]{0:T(512)(128)(4,1)S(1)} %get-tuple-element.99, f32[512]{0:T(512)S(1)} %gather_fusion.29, pred[512]{0:T(512)(128)(4,1)S(1)} %get-tuple-element.97, pred[512]{0:T(512)(128)(4,1)S(1)} %get-tuple-element.96, pred[512]{0:T(512)(128)(4,1)S(1)} %get-tuple-element.95, pred[512]{0:T(512)(128)(4,1)S(1)} %get-tuple-element.94, ...), kind=kLoop, calls=%fused_computation.681 | loop fusion | flops 34304 | bytes 37121 | tf_op jit(solution)/shard_map/jit(_where)/select_n | solution.py:201
  1186.9 71.9 %scatter_fusion.14 = f32[125,256]{1,0:T(8,128)} fusion(f32[125,256]{1,0:T(8,128)} %copy.1391, s32[576]{0:T(1024)S(1)} %fusion.42, f32[576]{0:T(1024)S(1)} %pad_maximum_fusion.17), kind=kCustom, calls=%fused_computation.86 | custom fusion | flops 576 | bytes 11520 | tf_op jit(solution)/shard_map/scatter-add | solution.py:204
  1299.7 5.1 collective-permute-done.125
  1361.8 39.7 %fusion.245 = f32[512]{0:T(512)S(1)} fusion(pred[512]{0:T(512)(128)(4,1)S(1)} %get-tuple-element.99, f32[512]{0:T(512)S(1)} %gather_fusion.34, pred[512]{0:T(512)(128)(4,1)S(1)} %get-tuple-element.97, pred[512]{0:T(512)(128)(4,1)S(1)} %get-tuple-element.96, pred[512]{0:T(512)(128)(4,1)S(1)} %get-tuple-element.95, pred[512]{0:T(512)(128)(4,1)S(1)} %get-tuple-element.94, ...), kind=kLoop, calls=%fused_computation.677 | loop fusion | flops 34304 | bytes 37121 | tf_op jit(solution)/shard_map/jit(_where)/select_n | solution.py:201
  1401.5 71.9 %scatter_fusion.16 = f32[125,256]{1,0:T(8,128)} fusion(f32[125,256]{1,0:T(8,128)} %copy.1412, s32[576]{0:T(1024)S(1)} %fusion.42, f32[576]{0:T(1024)S(1)} %pad_maximum_fusion.18), kind=kCustom, calls=%fused_computation.90 | custom fusion | flops 576 | bytes 11520 | tf_op jit(solution)/shard_map/scatter-add | solution.py:204
  1514.4 5.0 collective-permute-done.145
  1576.6 39.7 %fusion.242 = f32[512]{0:T(512)S(1)} fusion(pred[512]{0:T(512)(128)(4,1)S(1)} %get-tuple-element.99, f32[512]{0:T(512)S(1)} %gather_fusion.39, pred[512]{0:T(512)(128)(4,1)S(1)} %get-tuple-element.97, pred[512]{0:T(512)(128)(4,1)S(1)} %get-tuple-element.96, pred[512]{0:T(512)(128)(4,1)S(1)} %get-tuple-element.95, pred[512]{0:T(512)(128)(4,1)S(1)} %get-tuple-element.94, ...), kind=kLoop, calls=%fused_computation.673 | loop fusion | flops 34304 | bytes 37121 | tf_op jit(solution)/shard_map/jit(_where)/select_n | solution.py:201
  1616.2 71.9 %scatter_fusion.18 = f32[125,256]{1,0:T(8,128)} fusion(f32[125,256]{1,0:T(8,128)} %copy.1433, s32[576]{0:T(1024)S(1)} %fusion.42, f32[576]{0:T(1024)S(1)} %pad_maximum_fusion.19), kind=kCustom, calls=%fused_computation.94 | custom fusion | flops 576 | bytes 11520 | tf_op jit(solution)/shard_map/scatter-add | solution.py:204
  1729.1 5.1 collective-permute-done.165
  1791.1 39.7 %fusion.239 = f32[512]{0:T(512)S(1)} fusion(pred[512]{0:T(512)(128)(4,1)S(1)} %get-tuple-element.99, f32[512]{0:T(512)S(1)} %gather_fusion.44, pred[512]{0:T(512)(128)(4,1)S(1)} %get-tuple-element.97, pred[512]{0:T(512)(128)(4,1)S(1)} %get-tuple-element.96, pred[512]{0:T(512)(128)(4,1)S(1)} %get-tuple-element.95, pred[512]{0:T(512)(128)(4,1)S(1)} %get-tuple-element.94, ...), kind=kLoop, calls=%fused_computation.669 | loop fusion | flops 34304 | bytes 37121 | tf_op jit(solution)/shard_map/jit(_where)/select_n | solution.py:201
  1830.8 71.9 %scatter_fusion.20 = f32[125,256]{1,0:T(8,128)} fusion(f32[125,256]{1,0:T(8,128)} %copy.1454, s32[576]{0:T(1024)S(1)} %fusion.42, f32[576]{0:T(1024)S(1)} %pad_maximum_fusion.20), kind=kCustom, calls=%fused_computation.98 | custom fusion | flops 576 | bytes 11520 | tf_op jit(solution)/shard_map/scatter-add | solution.py:204
  1943.7 5.0 collective-permute-done.185
  2005.7 39.7 %fusion.236 = f32[512]{0:T(512)S(1)} fusion(pred[512]{0:T(512)(128)(4,1)S(1)} %get-tuple-element.99, f32[512]{0:T(512)S(1)} %gather_fusion.49, pred[512]{0:T(512)(128)(4,1)S(1)} %get-tuple-element.97, pred[512]{0:T(512)(128)(4,1)S(1)} %get-tuple-element.96, pred[512]{0:T(512)(128)(4,1)S(1)} %get-tuple-element.95, pred[512]{0:T(512)(128)(4,1)S(1)} %get-tuple-element.94, ...), kind=kLoop, calls=%fused_computation.665 | loop fusion | flops 34304 | bytes 37121 | tf_op jit(solution)/shard_map/jit(_where)/select_n | solution.py:201
  2045.5 71.9 %scatter_fusion.22 = f32[125,256]{1,0:T(8,128)} fusion(f32[125,256]{1,0:T(8,128)} %copy.1475, s32[576]{0:T(1024)S(1)} %fusion.42, f32[576]{0:T(1024)S(1)} %pad_maximum_fusion.21), kind=kCustom, calls=%fused_computation.102 | custom fusion | flops 576 | bytes 11520 | tf_op jit(solution)/shard_map/scatter-add | solution.py:204
  2158.3 5.0 collective-permute-done.205
  2220.4 39.8 %fusion.233 = f32[512]{0:T(512)S(1)} fusion(pred[512]{0:T(512)(128)(4,1)S(1)} %get-tuple-element.99, f32[512]{0:T(512)S(1)} %gather_fusion.54, pred[512]{0:T(512)(128)(4,1)S(1)} %get-tuple-element.97, pred[512]{0:T(512)(128)(4,1)S(1)} %get-tuple-element.96, pred[512]{0:T(512)(128)(4,1)S(1)} %get-tuple-element.95, pred[512]{0:T(512)(128)(4,1)S(1)} %get-tuple-element.94, ...), kind=kLoop, calls=%fused_computation.661 | loop fusion | flops 34304 | bytes 37121 | tf_op jit(solution)/shard_map/jit(_where)/select_n | solution.py:201
  2260.2 71.9 %scatter_fusion.24 = f32[125,256]{1,0:T(8,128)} fusion(f32[125,256]{1,0:T(8,128)} %copy.1496, s32[576]{0:T(1024)S(1)} %fusion.42, f32[576]{0:T(1024)S(1)} %pad_maximum_fusion.22), kind=kCustom, calls=%fused_computation.106 | custom fusion | flops 576 | bytes 11520 | tf_op jit(solution)/shard_map/scatter-add | solution.py:204
  2370.1 5.7 collective-permute-done.225
  2375.9 6.2 collective-permute-done.226
  2387.0 5.3 collective-permute-done.228
  2397.2 5.3 collective-permute-done.230
  2425.8 40.0 %fusion.230 = f32[512]{0:T(512)S(1)} fusion(pred[512]{0:T(512)(128)(4,1)S(1)} %get-tuple-element.99, f32[512]{0:T(512)S(1)} %gather_fusion.59, pred[512]{0:T(512)(128)(4,1)S(1)} %get-tuple-element.97, pred[512]{0:T(512)(128)(4,1)S(1)} %get-tuple-element.96, pred[512]{0:T(512)(128)(4,1)S(1)} %get-tuple-element.95, pred[512]{0:T(512)(128)(4,1)S(1)} %get-tuple-element.94, ...), kind=kLoop, calls=%fused_computation.657 | loop fusion | flops 34304 | bytes 37121 | tf_op jit(solution)/shard_map/jit(_where)/select_n | solution.py:201
  2465.9 30.1 %scatter_fusion.26 = f32[125,256]{1,0:T(8,128)S(1)} fusion(f32[125,256]{1,0:T(8,128)S(1)} %copy.1517, s32[576]{0:T(1024)S(1)} %fusion.42, f32[576]{0:T(1024)S(1)} %pad_maximum_fusion.23), kind=kCustom, calls=%fused_computation.110 | custom fusion | flops 576 | bytes 11520 | tf_op jit(solution)/shard_map/scatter-add | solution.py:204
  (1136 shorter events, 1099.1 us)
Async XLA Ops:
  113.4 56.7 %collective-permute-start.19 = (f32[1,4,1]{0,1,2:T(4,128)S(1)}, f32[1,4,1]{0,1,2:T(4,128)S(1)}, u32[]{:S(2)}, u32[]{:S(2)}) collective-permute-start(f32[1,4,1]{0,1,2:T(4,128)S(1)} %get-tuple-element.324), channel_id=1, source_target_pairs={{0,15},{1,0},{2,1},{3,2},{4,3},{5,4},{6,5},{7,6},{8,7},{9,8},{10,9... | collective-permute-start | bytes 56 | tf_op jit(solution)/shard_map/ppermute | solution.py:192
  114.9 55.1 %collective-permute-start.18 = (f32[1,4,1]{0,1,2:T(4,128)S(1)}, f32[1,4,1]{0,1,2:T(4,128)S(1)}, u32[]{:S(2)}, u32[]{:S(2)}) collective-permute-start(f32[1,4,1]{0,1,2:T(4,128)S(1)} %get-tuple-element.325), channel_id=1, source_target_pairs={{0,14},{1,15},{2,0},{3,1},{4,2},{5,3},{6,4},{7,5},{8,6},{9,7},{10,... | collective-permute-start | bytes 56 | tf_op jit(solution)/shard_map/ppermute | solution.py:192
  116.4 53.5 %collective-permute-start.17 = (f32[1,4,1]{0,1,2:T(4,128)S(1)}, f32[1,4,1]{0,1,2:T(4,128)S(1)}, u32[]{:S(2)}, u32[]{:S(2)}) collective-permute-start(f32[1,4,1]{0,1,2:T(4,128)S(1)} %get-tuple-element.326), channel_id=1, source_target_pairs={{0,13},{1,14},{2,15},{3,0},{4,1},{5,2},{6,3},{7,4},{8,5},{9,6},{10... | collective-permute-start | bytes 56 | tf_op jit(solution)/shard_map/ppermute | solution.py:192
  116.7 53.1 %collective-permute-start.16 = (f32[1,4,1]{0,1,2:T(4,128)S(1)}, f32[1,4,1]{0,1,2:T(4,128)S(1)}, u32[]{:S(2)}, u32[]{:S(2)}) collective-permute-start(f32[1,4,1]{0,1,2:T(4,128)S(1)} %get-tuple-element.327), channel_id=1, source_target_pairs={{0,12},{1,13},{2,14},{3,15},{4,0},{5,1},{6,2},{7,3},{8,4},{9,5},{1... | collective-permute-start | bytes 56 | tf_op jit(solution)/shard_map/ppermute | solution.py:192
  272.3 56.9 %collective-permute-start.39 = (f32[1,4,1]{0,1,2:T(4,128)S(1)}, f32[1,4,1]{0,1,2:T(4,128)S(1)}, u32[]{:S(2)}, u32[]{:S(2)}) collective-permute-start(f32[1,4,1]{0,1,2:T(4,128)S(1)} %get-tuple-element.309), channel_id=1, source_target_pairs={{0,15},{1,0},{2,1},{3,2},{4,3},{5,4},{6,5},{7,6},{8,7},{9,8},{10,9... | collective-permute-start | bytes 56 | tf_op jit(solution)/shard_map/ppermute | solution.py:192
  272.4 56.7 %collective-permute-start.38 = (f32[1,4,1]{0,1,2:T(4,128)S(1)}, f32[1,4,1]{0,1,2:T(4,128)S(1)}, u32[]{:S(2)}, u32[]{:S(2)}) collective-permute-start(f32[1,4,1]{0,1,2:T(4,128)S(1)} %get-tuple-element.310), channel_id=1, source_target_pairs={{0,14},{1,15},{2,0},{3,1},{4,2},{5,3},{6,4},{7,5},{8,6},{9,7},{10,... | collective-permute-start | bytes 56 | tf_op jit(solution)/shard_map/ppermute | solution.py:192
  273.7 55.2 %collective-permute-start.37 = (f32[1,4,1]{0,1,2:T(4,128)S(1)}, f32[1,4,1]{0,1,2:T(4,128)S(1)}, u32[]{:S(2)}, u32[]{:S(2)}) collective-permute-start(f32[1,4,1]{0,1,2:T(4,128)S(1)} %get-tuple-element.311), channel_id=1, source_target_pairs={{0,13},{1,14},{2,15},{3,0},{4,1},{5,2},{6,3},{7,4},{8,5},{9,6},{10... | collective-permute-start | bytes 56 | tf_op jit(solution)/shard_map/ppermute | solution.py:192
  275.2 53.7 %collective-permute-start.36 = (f32[1,4,1]{0,1,2:T(4,128)S(1)}, f32[1,4,1]{0,1,2:T(4,128)S(1)}, u32[]{:S(2)}, u32[]{:S(2)}) collective-permute-start(f32[1,4,1]{0,1,2:T(4,128)S(1)} %get-tuple-element.312), channel_id=1, source_target_pairs={{0,12},{1,13},{2,14},{3,15},{4,0},{5,1},{6,2},{7,3},{8,4},{9,5},{1... | collective-permute-start | bytes 56 | tf_op jit(solution)/shard_map/ppermute | solution.py:192
  437.0 61.8 %collective-permute-start.59 = (f32[1,4,1]{0,1,2:T(4,128)S(1)}, f32[1,4,1]{0,1,2:T(4,128)S(1)}, u32[]{:S(2)}, u32[]{:S(2)}) collective-permute-start(f32[1,4,1]{0,1,2:T(4,128)S(1)} %get-tuple-element.294), channel_id=1, source_target_pairs={{0,15},{1,0},{2,1},{3,2},{4,3},{5,4},{6,5},{7,6},{8,7},{9,8},{10,9... | collective-permute-start | bytes 56 | tf_op jit(solution)/shard_map/ppermute | solution.py:192
  437.4 60.0 %collective-permute-start.58 = (f32[1,4,1]{0,1,2:T(4,128)S(1)}, f32[1,4,1]{0,1,2:T(4,128)S(1)}, u32[]{:S(2)}, u32[]{:S(2)}) collective-permute-start(f32[1,4,1]{0,1,2:T(4,128)S(1)} %get-tuple-element.295), channel_id=1, source_target_pairs={{0,14},{1,15},{2,0},{3,1},{4,2},{5,3},{6,4},{7,5},{8,6},{9,7},{10,... | collective-permute-start | bytes 56 | tf_op jit(solution)/shard_map/ppermute | solution.py:192
  438.4 57.7 %collective-permute-start.57 = (f32[1,4,1]{0,1,2:T(4,128)S(1)}, f32[1,4,1]{0,1,2:T(4,128)S(1)}, u32[]{:S(2)}, u32[]{:S(2)}) collective-permute-start(f32[1,4,1]{0,1,2:T(4,128)S(1)} %get-tuple-element.296), channel_id=1, source_target_pairs={{0,13},{1,14},{2,15},{3,0},{4,1},{5,2},{6,3},{7,4},{8,5},{9,6},{10... | collective-permute-start | bytes 56 | tf_op jit(solution)/shard_map/ppermute | solution.py:192
  439.9 54.9 %collective-permute-start.56 = (f32[1,4,1]{0,1,2:T(4,128)S(1)}, f32[1,4,1]{0,1,2:T(4,128)S(1)}, u32[]{:S(2)}, u32[]{:S(2)}) collective-permute-start(f32[1,4,1]{0,1,2:T(4,128)S(1)} %get-tuple-element.297), channel_id=1, source_target_pairs={{0,12},{1,13},{2,14},{3,15},{4,0},{5,1},{6,2},{7,3},{8,4},{9,5},{1... | collective-permute-start | bytes 56 | tf_op jit(solution)/shard_map/ppermute | solution.py:192
  651.3 61.8 %collective-permute-start.79 = (f32[1,4,1]{0,1,2:T(4,128)S(1)}, f32[1,4,1]{0,1,2:T(4,128)S(1)}, u32[]{:S(2)}, u32[]{:S(2)}) collective-permute-start(f32[1,4,1]{0,1,2:T(4,128)S(1)} %get-tuple-element.279), channel_id=1, source_target_pairs={{0,15},{1,0},{2,1},{3,2},{4,3},{5,4},{6,5},{7,6},{8,7},{9,8},{10,9... | collective-permute-start | bytes 56 | tf_op jit(solution)/shard_map/ppermute | solution.py:192
  651.7 60.1 %collective-permute-start.78 = (f32[1,4,1]{0,1,2:T(4,128)S(1)}, f32[1,4,1]{0,1,2:T(4,128)S(1)}, u32[]{:S(2)}, u32[]{:S(2)}) collective-permute-start(f32[1,4,1]{0,1,2:T(4,128)S(1)} %get-tuple-element.280), channel_id=1, source_target_pairs={{0,14},{1,15},{2,0},{3,1},{4,2},{5,3},{6,4},{7,5},{8,6},{9,7},{10,... | collective-permute-start | bytes 56 | tf_op jit(solution)/shard_map/ppermute | solution.py:192
  653.2 57.2 %collective-permute-start.77 = (f32[1,4,1]{0,1,2:T(4,128)S(1)}, f32[1,4,1]{0,1,2:T(4,128)S(1)}, u32[]{:S(2)}, u32[]{:S(2)}) collective-permute-start(f32[1,4,1]{0,1,2:T(4,128)S(1)} %get-tuple-element.281), channel_id=1, source_target_pairs={{0,13},{1,14},{2,15},{3,0},{4,1},{5,2},{6,3},{7,4},{8,5},{9,6},{10... | collective-permute-start | bytes 56 | tf_op jit(solution)/shard_map/ppermute | solution.py:192
  654.2 54.9 %collective-permute-start.76 = (f32[1,4,1]{0,1,2:T(4,128)S(1)}, f32[1,4,1]{0,1,2:T(4,128)S(1)}, u32[]{:S(2)}, u32[]{:S(2)}) collective-permute-start(f32[1,4,1]{0,1,2:T(4,128)S(1)} %get-tuple-element.282), channel_id=1, source_target_pairs={{0,12},{1,13},{2,14},{3,15},{4,0},{5,1},{6,2},{7,3},{8,4},{9,5},{1... | collective-permute-start | bytes 56 | tf_op jit(solution)/shard_map/ppermute | solution.py:192
  865.8 61.8 %collective-permute-start.99 = (f32[1,4,1]{0,1,2:T(4,128)S(1)}, f32[1,4,1]{0,1,2:T(4,128)S(1)}, u32[]{:S(2)}, u32[]{:S(2)}) collective-permute-start(f32[1,4,1]{0,1,2:T(4,128)S(1)} %get-tuple-element.264), channel_id=1, source_target_pairs={{0,15},{1,0},{2,1},{3,2},{4,3},{5,4},{6,5},{7,6},{8,7},{9,8},{10,9... | collective-permute-start | bytes 56 | tf_op jit(solution)/shard_map/ppermute | solution.py:192
  866.2 60.0 %collective-permute-start.98 = (f32[1,4,1]{0,1,2:T(4,128)S(1)}, f32[1,4,1]{0,1,2:T(4,128)S(1)}, u32[]{:S(2)}, u32[]{:S(2)}) collective-permute-start(f32[1,4,1]{0,1,2:T(4,128)S(1)} %get-tuple-element.265), channel_id=1, source_target_pairs={{0,14},{1,15},{2,0},{3,1},{4,2},{5,3},{6,4},{7,5},{8,6},{9,7},{10,... | collective-permute-start | bytes 56 | tf_op jit(solution)/shard_map/ppermute | solution.py:192
  867.6 57.2 %collective-permute-start.97 = (f32[1,4,1]{0,1,2:T(4,128)S(1)}, f32[1,4,1]{0,1,2:T(4,128)S(1)}, u32[]{:S(2)}, u32[]{:S(2)}) collective-permute-start(f32[1,4,1]{0,1,2:T(4,128)S(1)} %get-tuple-element.266), channel_id=1, source_target_pairs={{0,13},{1,14},{2,15},{3,0},{4,1},{5,2},{6,3},{7,4},{8,5},{9,6},{10... | collective-permute-start | bytes 56 | tf_op jit(solution)/shard_map/ppermute | solution.py:192
  868.6 54.9 %collective-permute-start.96 = (f32[1,4,1]{0,1,2:T(4,128)S(1)}, f32[1,4,1]{0,1,2:T(4,128)S(1)}, u32[]{:S(2)}, u32[]{:S(2)}) collective-permute-start(f32[1,4,1]{0,1,2:T(4,128)S(1)} %get-tuple-element.267), channel_id=1, source_target_pairs={{0,12},{1,13},{2,14},{3,15},{4,0},{5,1},{6,2},{7,3},{8,4},{9,5},{1... | collective-permute-start | bytes 56 | tf_op jit(solution)/shard_map/ppermute | solution.py:192
  1080.4 61.8 %collective-permute-start.119 = (f32[1,4,1]{0,1,2:T(4,128)S(1)}, f32[1,4,1]{0,1,2:T(4,128)S(1)}, u32[]{:S(2)}, u32[]{:S(2)}) collective-permute-start(f32[1,4,1]{0,1,2:T(4,128)S(1)} %get-tuple-element.249), channel_id=1, source_target_pairs={{0,15},{1,0},{2,1},{3,2},{4,3},{5,4},{6,5},{7,6},{8,7},{9,8},{10,9... | collective-permute-start | bytes 56 | tf_op jit(solution)/shard_map/ppermute | solution.py:192
  1080.7 60.2 %collective-permute-start.118 = (f32[1,4,1]{0,1,2:T(4,128)S(1)}, f32[1,4,1]{0,1,2:T(4,128)S(1)}, u32[]{:S(2)}, u32[]{:S(2)}) collective-permute-start(f32[1,4,1]{0,1,2:T(4,128)S(1)} %get-tuple-element.250), channel_id=1, source_target_pairs={{0,14},{1,15},{2,0},{3,1},{4,2},{5,3},{6,4},{7,5},{8,6},{9,7},{10,... | collective-permute-start | bytes 56 | tf_op jit(solution)/shard_map/ppermute | solution.py:192
  1082.3 57.2 %collective-permute-start.117 = (f32[1,4,1]{0,1,2:T(4,128)S(1)}, f32[1,4,1]{0,1,2:T(4,128)S(1)}, u32[]{:S(2)}, u32[]{:S(2)}) collective-permute-start(f32[1,4,1]{0,1,2:T(4,128)S(1)} %get-tuple-element.251), channel_id=1, source_target_pairs={{0,13},{1,14},{2,15},{3,0},{4,1},{5,2},{6,3},{7,4},{8,5},{9,6},{10... | collective-permute-start | bytes 56 | tf_op jit(solution)/shard_map/ppermute | solution.py:192
  1083.3 54.9 %collective-permute-start.116 = (f32[1,4,1]{0,1,2:T(4,128)S(1)}, f32[1,4,1]{0,1,2:T(4,128)S(1)}, u32[]{:S(2)}, u32[]{:S(2)}) collective-permute-start(f32[1,4,1]{0,1,2:T(4,128)S(1)} %get-tuple-element.252), channel_id=1, source_target_pairs={{0,12},{1,13},{2,14},{3,15},{4,0},{5,1},{6,2},{7,3},{8,4},{9,5},{1... | collective-permute-start | bytes 56 | tf_op jit(solution)/shard_map/ppermute | solution.py:192
  1294.8 61.8 %collective-permute-start.139 = (f32[1,4,1]{0,1,2:T(4,128)S(1)}, f32[1,4,1]{0,1,2:T(4,128)S(1)}, u32[]{:S(2)}, u32[]{:S(2)}) collective-permute-start(f32[1,4,1]{0,1,2:T(4,128)S(1)} %get-tuple-element.234), channel_id=1, source_target_pairs={{0,15},{1,0},{2,1},{3,2},{4,3},{5,4},{6,5},{7,6},{8,7},{9,8},{10,9... | collective-permute-start | bytes 56 | tf_op jit(solution)/shard_map/ppermute | solution.py:192
  1295.2 60.1 %collective-permute-start.138 = (f32[1,4,1]{0,1,2:T(4,128)S(1)}, f32[1,4,1]{0,1,2:T(4,128)S(1)}, u32[]{:S(2)}, u32[]{:S(2)}) collective-permute-start(f32[1,4,1]{0,1,2:T(4,128)S(1)} %get-tuple-element.235), channel_id=1, source_target_pairs={{0,14},{1,15},{2,0},{3,1},{4,2},{5,3},{6,4},{7,5},{8,6},{9,7},{10,... | collective-permute-start | bytes 56 | tf_op jit(solution)/shard_map/ppermute | solution.py:192
  1296.7 57.2 %collective-permute-start.137 = (f32[1,4,1]{0,1,2:T(4,128)S(1)}, f32[1,4,1]{0,1,2:T(4,128)S(1)}, u32[]{:S(2)}, u32[]{:S(2)}) collective-permute-start(f32[1,4,1]{0,1,2:T(4,128)S(1)} %get-tuple-element.236), channel_id=1, source_target_pairs={{0,13},{1,14},{2,15},{3,0},{4,1},{5,2},{6,3},{7,4},{8,5},{9,6},{10... | collective-permute-start | bytes 56 | tf_op jit(solution)/shard_map/ppermute | solution.py:192
  1297.7 54.9 %collective-permute-start.136 = (f32[1,4,1]{0,1,2:T(4,128)S(1)}, f32[1,4,1]{0,1,2:T(4,128)S(1)}, u32[]{:S(2)}, u32[]{:S(2)}) collective-permute-start(f32[1,4,1]{0,1,2:T(4,128)S(1)} %get-tuple-element.237), channel_id=1, source_target_pairs={{0,12},{1,13},{2,14},{3,15},{4,0},{5,1},{6,2},{7,3},{8,4},{9,5},{1... | collective-permute-start | bytes 56 | tf_op jit(solution)/shard_map/ppermute | solution.py:192
  1509.4 61.8 %collective-permute-start.159 = (f32[1,4,1]{0,1,2:T(4,128)S(1)}, f32[1,4,1]{0,1,2:T(4,128)S(1)}, u32[]{:S(2)}, u32[]{:S(2)}) collective-permute-start(f32[1,4,1]{0,1,2:T(4,128)S(1)} %get-tuple-element.219), channel_id=1, source_target_pairs={{0,15},{1,0},{2,1},{3,2},{4,3},{5,4},{6,5},{7,6},{8,7},{9,8},{10,9... | collective-permute-start | bytes 56 | tf_op jit(solution)/shard_map/ppermute | solution.py:192
  1509.8 60.0 %collective-permute-start.158 = (f32[1,4,1]{0,1,2:T(4,128)S(1)}, f32[1,4,1]{0,1,2:T(4,128)S(1)}, u32[]{:S(2)}, u32[]{:S(2)}) collective-permute-start(f32[1,4,1]{0,1,2:T(4,128)S(1)} %get-tuple-element.220), channel_id=1, source_target_pairs={{0,14},{1,15},{2,0},{3,1},{4,2},{5,3},{6,4},{7,5},{8,6},{9,7},{10,... | collective-permute-start | bytes 56 | tf_op jit(solution)/shard_map/ppermute | solution.py:192
  1511.3 57.2 %collective-permute-start.157 = (f32[1,4,1]{0,1,2:T(4,128)S(1)}, f32[1,4,1]{0,1,2:T(4,128)S(1)}, u32[]{:S(2)}, u32[]{:S(2)}) collective-permute-start(f32[1,4,1]{0,1,2:T(4,128)S(1)} %get-tuple-element.221), channel_id=1, source_target_pairs={{0,13},{1,14},{2,15},{3,0},{4,1},{5,2},{6,3},{7,4},{8,5},{9,6},{10... | collective-permute-start | bytes 56 | tf_op jit(solution)/shard_map/ppermute | solution.py:192
  1512.3 54.9 %collective-permute-start.156 = (f32[1,4,1]{0,1,2:T(4,128)S(1)}, f32[1,4,1]{0,1,2:T(4,128)S(1)}, u32[]{:S(2)}, u32[]{:S(2)}) collective-permute-start(f32[1,4,1]{0,1,2:T(4,128)S(1)} %get-tuple-element.222), channel_id=1, source_target_pairs={{0,12},{1,13},{2,14},{3,15},{4,0},{5,1},{6,2},{7,3},{8,4},{9,5},{1... | collective-permute-start | bytes 56 | tf_op jit(solution)/shard_map/ppermute | solution.py:192
  1724.2 61.8 %collective-permute-start.179 = (f32[1,4,1]{0,1,2:T(4,128)S(1)}, f32[1,4,1]{0,1,2:T(4,128)S(1)}, u32[]{:S(2)}, u32[]{:S(2)}) collective-permute-start(f32[1,4,1]{0,1,2:T(4,128)S(1)} %get-tuple-element.204), channel_id=1, source_target_pairs={{0,15},{1,0},{2,1},{3,2},{4,3},{5,4},{6,5},{7,6},{8,7},{9,8},{10,9... | collective-permute-start | bytes 56 | tf_op jit(solution)/shard_map/ppermute | solution.py:192
  1724.6 60.1 %collective-permute-start.178 = (f32[1,4,1]{0,1,2:T(4,128)S(1)}, f32[1,4,1]{0,1,2:T(4,128)S(1)}, u32[]{:S(2)}, u32[]{:S(2)}) collective-permute-start(f32[1,4,1]{0,1,2:T(4,128)S(1)} %get-tuple-element.205), channel_id=1, source_target_pairs={{0,14},{1,15},{2,0},{3,1},{4,2},{5,3},{6,4},{7,5},{8,6},{9,7},{10,... | collective-permute-start | bytes 56 | tf_op jit(solution)/shard_map/ppermute | solution.py:192
  1726.1 57.2 %collective-permute-start.177 = (f32[1,4,1]{0,1,2:T(4,128)S(1)}, f32[1,4,1]{0,1,2:T(4,128)S(1)}, u32[]{:S(2)}, u32[]{:S(2)}) collective-permute-start(f32[1,4,1]{0,1,2:T(4,128)S(1)} %get-tuple-element.206), channel_id=1, source_target_pairs={{0,13},{1,14},{2,15},{3,0},{4,1},{5,2},{6,3},{7,4},{8,5},{9,6},{10... | collective-permute-start | bytes 56 | tf_op jit(solution)/shard_map/ppermute | solution.py:192
  1727.1 54.9 %collective-permute-start.176 = (f32[1,4,1]{0,1,2:T(4,128)S(1)}, f32[1,4,1]{0,1,2:T(4,128)S(1)}, u32[]{:S(2)}, u32[]{:S(2)}) collective-permute-start(f32[1,4,1]{0,1,2:T(4,128)S(1)} %get-tuple-element.207), channel_id=1, source_target_pairs={{0,12},{1,13},{2,14},{3,15},{4,0},{5,1},{6,2},{7,3},{8,4},{9,5},{1... | collective-permute-start | bytes 56 | tf_op jit(solution)/shard_map/ppermute | solution.py:192
  1938.7 61.8 %collective-permute-start.199 = (f32[1,4,1]{0,1,2:T(4,128)S(1)}, f32[1,4,1]{0,1,2:T(4,128)S(1)}, u32[]{:S(2)}, u32[]{:S(2)}) collective-permute-start(f32[1,4,1]{0,1,2:T(4,128)S(1)} %get-tuple-element.189), channel_id=1, source_target_pairs={{0,15},{1,0},{2,1},{3,2},{4,3},{5,4},{6,5},{7,6},{8,7},{9,8},{10,9... | collective-permute-start | bytes 56 | tf_op jit(solution)/shard_map/ppermute | solution.py:192
  1939.2 60.0 %collective-permute-start.198 = (f32[1,4,1]{0,1,2:T(4,128)S(1)}, f32[1,4,1]{0,1,2:T(4,128)S(1)}, u32[]{:S(2)}, u32[]{:S(2)}) collective-permute-start(f32[1,4,1]{0,1,2:T(4,128)S(1)} %get-tuple-element.190), channel_id=1, source_target_pairs={{0,14},{1,15},{2,0},{3,1},{4,2},{5,3},{6,4},{7,5},{8,6},{9,7},{10,... | collective-permute-start | bytes 56 | tf_op jit(solution)/shard_map/ppermute | solution.py:192
  1940.6 57.2 %collective-permute-start.197 = (f32[1,4,1]{0,1,2:T(4,128)S(1)}, f32[1,4,1]{0,1,2:T(4,128)S(1)}, u32[]{:S(2)}, u32[]{:S(2)}) collective-permute-start(f32[1,4,1]{0,1,2:T(4,128)S(1)} %get-tuple-element.191), channel_id=1, source_target_pairs={{0,13},{1,14},{2,15},{3,0},{4,1},{5,2},{6,3},{7,4},{8,5},{9,6},{10... | collective-permute-start | bytes 56 | tf_op jit(solution)/shard_map/ppermute | solution.py:192
  1941.6 54.9 %collective-permute-start.196 = (f32[1,4,1]{0,1,2:T(4,128)S(1)}, f32[1,4,1]{0,1,2:T(4,128)S(1)}, u32[]{:S(2)}, u32[]{:S(2)}) collective-permute-start(f32[1,4,1]{0,1,2:T(4,128)S(1)} %get-tuple-element.192), channel_id=1, source_target_pairs={{0,12},{1,13},{2,14},{3,15},{4,0},{5,1},{6,2},{7,3},{8,4},{9,5},{1... | collective-permute-start | bytes 56 | tf_op jit(solution)/shard_map/ppermute | solution.py:192
  2153.4 61.8 %collective-permute-start.219 = (f32[1,4,1]{0,1,2:T(4,128)S(1)}, f32[1,4,1]{0,1,2:T(4,128)S(1)}, u32[]{:S(2)}, u32[]{:S(2)}) collective-permute-start(f32[1,4,1]{0,1,2:T(4,128)S(1)} %get-tuple-element.174), channel_id=1, source_target_pairs={{0,15},{1,0},{2,1},{3,2},{4,3},{5,4},{6,5},{7,6},{8,7},{9,8},{10,9... | collective-permute-start | bytes 56 | tf_op jit(solution)/shard_map/ppermute | solution.py:192
  2153.8 60.0 %collective-permute-start.218 = (f32[1,4,1]{0,1,2:T(4,128)S(1)}, f32[1,4,1]{0,1,2:T(4,128)S(1)}, u32[]{:S(2)}, u32[]{:S(2)}) collective-permute-start(f32[1,4,1]{0,1,2:T(4,128)S(1)} %get-tuple-element.175), channel_id=1, source_target_pairs={{0,14},{1,15},{2,0},{3,1},{4,2},{5,3},{6,4},{7,5},{8,6},{9,7},{10,... | collective-permute-start | bytes 56 | tf_op jit(solution)/shard_map/ppermute | solution.py:192
  2155.3 57.2 %collective-permute-start.217 = (f32[1,4,1]{0,1,2:T(4,128)S(1)}, f32[1,4,1]{0,1,2:T(4,128)S(1)}, u32[]{:S(2)}, u32[]{:S(2)}) collective-permute-start(f32[1,4,1]{0,1,2:T(4,128)S(1)} %get-tuple-element.176), channel_id=1, source_target_pairs={{0,13},{1,14},{2,15},{3,0},{4,1},{5,2},{6,3},{7,4},{8,5},{9,6},{10... | collective-permute-start | bytes 56 | tf_op jit(solution)/shard_map/ppermute | solution.py:192
  2156.3 54.9 %collective-permute-start.216 = (f32[1,4,1]{0,1,2:T(4,128)S(1)}, f32[1,4,1]{0,1,2:T(4,128)S(1)}, u32[]{:S(2)}, u32[]{:S(2)}) collective-permute-start(f32[1,4,1]{0,1,2:T(4,128)S(1)} %get-tuple-element.177), channel_id=1, source_target_pairs={{0,12},{1,13},{2,14},{3,15},{4,0},{5,1},{6,2},{7,3},{8,4},{9,5},{1... | collective-permute-start | bytes 56 | tf_op jit(solution)/shard_map/ppermute | solution.py:192
  2365.9 56.9 %collective-permute-start.239 = (f32[1,4,1]{0,1,2:T(4,128)S(1)}, f32[1,4,1]{0,1,2:T(4,128)S(1)}, u32[]{:S(2)}, u32[]{:S(2)}) collective-permute-start(f32[1,4,1]{0,1,2:T(4,128)S(1)} %get-tuple-element.159), channel_id=1, source_target_pairs={{0,15},{1,0},{2,1},{3,2},{4,3},{5,4},{6,5},{7,6},{8,7},{9,8},{10,9... | collective-permute-start | bytes 56 | tf_op jit(solution)/shard_map/ppermute | solution.py:192
  2365.9 56.7 %collective-permute-start.238 = (f32[1,4,1]{0,1,2:T(4,128)S(1)}, f32[1,4,1]{0,1,2:T(4,128)S(1)}, u32[]{:S(2)}, u32[]{:S(2)}) collective-permute-start(f32[1,4,1]{0,1,2:T(4,128)S(1)} %get-tuple-element.160), channel_id=1, source_target_pairs={{0,14},{1,15},{2,0},{3,1},{4,2},{5,3},{6,4},{7,5},{8,6},{9,7},{10,... | collective-permute-start | bytes 56 | tf_op jit(solution)/shard_map/ppermute | solution.py:192
  2367.8 54.8 %collective-permute-start.237 = (f32[1,4,1]{0,1,2:T(4,128)S(1)}, f32[1,4,1]{0,1,2:T(4,128)S(1)}, u32[]{:S(2)}, u32[]{:S(2)}) collective-permute-start(f32[1,4,1]{0,1,2:T(4,128)S(1)} %get-tuple-element.161), channel_id=1, source_target_pairs={{0,13},{1,14},{2,15},{3,0},{4,1},{5,2},{6,3},{7,4},{8,5},{9,6},{10... | collective-permute-start | bytes 56 | tf_op jit(solution)/shard_map/ppermute | solution.py:192
  2368.8 53.7 %collective-permute-start.236 = (f32[1,4,1]{0,1,2:T(4,128)S(1)}, f32[1,4,1]{0,1,2:T(4,128)S(1)}, u32[]{:S(2)}, u32[]{:S(2)}) collective-permute-start(f32[1,4,1]{0,1,2:T(4,128)S(1)} %get-tuple-element.162), channel_id=1, source_target_pairs={{0,12},{1,13},{2,14},{3,15},{4,0},{5,1},{6,2},{7,3},{8,4},{9,5},{1... | collective-permute-start | bytes 56 | tf_op jit(solution)/shard_map/ppermute | solution.py:192
  (207 other events, 2141.8 us)
